TPU v7x, 256 devices: a whole 4x4x8 slice. The times are simulated.
256 devices in a mesh: row: 16 (over y, x), col: 16 (over z, core).
Axes of the slice: x: 4, y: 4, z: 8, core: 2. Of those that a mesh axis runs over, the one named last changes fastest.
Arguments:
- matrix: float32 [16384, 16384], P('row', 'col'), may hold values from 0 to 9.5, as said below
Outputs:
- factored: float32 [16384, 16384], P('row', 'col')
Inputs may be any that keep to these rules, and one draw needn't show every extreme that they name: `matrix`: symmetric positive definite once the block order is reverted.
All inputs are finite; a program needn't handle non-finite values.
Results may differ from a plain program's by a relative error of at most 0.0003.
Values sent between devices are 32-bit elements; how exact they have to be, the bound alone decides.
A program may use at most 128 MiB of HBM per device.

v0:
```python
import jax
import jax.numpy as jnp
from jax import lax
from jax.sharding import PartitionSpec as P

NB = 256
PANELS = 3


def from_root(shard, axis, root):
    mine = lax.axis_index(axis) == root
    return lax.psum(jnp.where(mine, shard, jnp.zeros_like(shard)), axis)


def solve_panel(factor, raw_rows):
    slots = raw_rows.shape[0]
    width = raw_rows.shape[1]
    flat = raw_rows.reshape(slots * width, width)
    solved = jax.scipy.linalg.solve_triangular(factor, flat.T, lower=True).T
    return solved.reshape(slots, width, width)


def subtract(part, panel_rows, column_rows):
    return part - jnp.einsum(
        "lan,mbn->lamb",
        panel_rows,
        column_rows,
        precision=lax.Precision.HIGHEST,
        preferred_element_type=jnp.float32,
    )


def body(matrix):
    grid_rows = lax.axis_size("row")
    grid_cols = lax.axis_size("col")
    row_slots = matrix.shape[0] // NB
    col_slots = matrix.shape[1] // NB
    stride = grid_cols // grid_rows
    my_row = lax.axis_index("row")
    my_col = lax.axis_index("col")
    blocks = matrix.reshape(row_slots, NB, col_slots, NB)
    row_ids = jnp.arange(row_slots, dtype=jnp.int32) * grid_rows + my_row
    col_ids = jnp.arange(col_slots, dtype=jnp.int32) * grid_cols + my_col
    carried = None
    for panel_at in range(PANELS):
        root_row = panel_at % grid_rows
        root_col = panel_at % grid_cols
        slot_row = panel_at // grid_rows
        slot_col = panel_at // grid_cols
        source = blocks[:, :, slot_col, :]
        below_mask = (row_ids > panel_at)[:, None, None]
        diag_block = from_root(source[slot_row], "row", root_row)
        factor = jnp.linalg.cholesky(diag_block)
        solved = jnp.where(below_mask, solve_panel(factor, source), 0.0)
        panel_rows = from_root(solved, "col", root_col)
        fetched = from_root(panel_rows, "row", my_col % grid_rows)
        column_rows = lax.dynamic_index_in_dim(
            fetched.reshape(col_slots, stride, NB, NB), my_col // grid_rows, 1, keepdims=False
        )
        owner_column = jnp.where((row_ids == panel_at)[:, None, None], factor[None], panel_rows)
        blocks = blocks.at[:, :, slot_col, :].set(
            jnp.where(my_col == root_col, owner_column, source)
        )
        blocks = subtract(blocks, panel_rows, column_rows)
        carried = None
    zero_mask = (row_ids[:, None] < col_ids[None, :]) & (row_ids[:, None] < PANELS)
    result = jnp.where(zero_mask[:, None, :, None], 0.0, blocks)
    return result.reshape(matrix.shape)


def solution(mesh):
    in_specs = (P("row", "col"),)
    out_specs = P("row", "col")
    return jax.shard_map(body, mesh=mesh, in_specs=in_specs, out_specs=out_specs, check_vma=False)
```

profile of v0, /device:TPU:32, one launch (start us, length us, event | category | flops | bytes accessed | tf_op | source)
XLA Modules:
  0.0 1180.5 jit_solution(10339150950592994072)
XLA Ops:
  6.5 5.6 reshape.239
  12.1 5.2 copy.29
  17.4 1.7 fusion.18
  19.1 2.9 slice.154
  22.2 94.0 %all-reduce.11.cloned.1.call-done = f32[256,256]{0,1:T(8,128)} async-done(((f32[256,256]{0,1:T(8,128)}), f32[256,256]{0,1:T(8,128)}) %all-reduce.11.cloned.1.call-update) | async-done | bytes 262160 | tf_op jit(solution)/shard_map/psum | solution.py:12
  118.2 11.7 cholesky.172
  130.0 9.8 custom-call.15
  140.3 11.7 cholesky.189
  154.1 4.2 while.9
  154.9 1.4 bitcast_dynamic-update-slice_fusion.7
  156.9 1.4 bitcast_dynamic-update-slice_fusion.7
  158.2 19.7 %custom-call.16 = f32[2,128,128]{1,2,0:T(8,128)S(1)} custom-call(f32[2,128,128]{2,1,0:T(8,128)S(1)} %get-tuple-element.63), custom_call_target="InvertDiagBlocksLowerTriangular" | custom-call | tf_op jit(solution)/shard_map/jit(_solve_triangular)/triangular_solve | solution.py:19
  182.3 108.2 %all-reduce.13.cloned.1.call-done = f32[4,256,256]{1,2,0:T(8,128)} async-done(((f32[4,256,256]{1,2,0:T(8,128)}), f32[4,256,256]{1,2,0:T(8,128)}) %all-reduce.13.cloned.1.call-update) | async-done | bytes 1048592 | tf_op jit(solution)/shard_map/psum | solution.py:12
  292.4 1.2 bitcast_dynamic-update-slice_fusion.3
  293.6 100.3 %all-reduce.15.cloned.1.call-done = f32[4,256,256]{1,2,0:T(8,128)} async-done(((f32[4,256,256]{1,2,0:T(8,128)}), f32[4,256,256]{1,2,0:T(8,128)}) %all-reduce.15.cloned.1.call-update) | async-done | bytes 1048592 | tf_op jit(solution)/shard_map/psum | solution.py:12
  393.9 5.8 convolution_subtract_fusion.1
  399.7 2.0 copy-done.1
  402.9 1.4 slice_bitcast_fusion.1
  404.7 91.4 %all-reduce.17.cloned.1.call-done = f32[256,256]{0,1:T(8,128)} async-done(((f32[256,256]{0,1:T(8,128)}), f32[256,256]{0,1:T(8,128)}) %all-reduce.17.cloned.1.call-update) | async-done | bytes 262160 | tf_op jit(solution)/shard_map/psum | solution.py:12
  498.2 11.7 cholesky.206
  510.0 9.8 custom-call.17
  520.3 11.7 cholesky.223
  534.7 4.2 while.10
  535.6 1.3 bitcast_dynamic-update-slice_fusion.8
  537.6 1.3 bitcast_dynamic-update-slice_fusion.8
  539.0 19.7 %custom-call.18 = f32[2,128,128]{1,2,0:T(8,128)S(1)} custom-call(f32[2,128,128]{2,1,0:T(8,128)S(1)} %get-tuple-element.64), custom_call_target="InvertDiagBlocksLowerTriangular" | custom-call | tf_op jit(solution)/shard_map/jit(_solve_triangular)/triangular_solve | solution.py:19
  561.7 1.2 select_select_fusion.1
  563.0 108.2 %all-reduce.19.cloned.1.call-done = f32[4,256,256]{1,2,0:T(8,128)} async-done(((f32[4,256,256]{1,2,0:T(8,128)}), f32[4,256,256]{1,2,0:T(8,128)}) %all-reduce.19.cloned.1.call-update) | async-done | bytes 1048592 | tf_op jit(solution)/shard_map/psum | solution.py:12
  672.8 1.2 fusion.3
  674.0 100.5 %all-reduce.21.cloned.1.call-done = f32[4,256,256]{1,2,0:T(8,128)} async-done(((f32[4,256,256]{1,2,0:T(8,128)}), f32[4,256,256]{1,2,0:T(8,128)}) %all-reduce.21.cloned.1.call-update) | async-done | bytes 1048592 | tf_op jit(solution)/shard_map/psum | solution.py:12
  774.5 5.8 convolution_subtract_fusion
  780.4 2.0 copy-done
  783.4 1.4 slice_bitcast_fusion
  785.1 91.7 %all-reduce.23.cloned.1.call-done = f32[256,256]{0,1:T(8,128)} async-done(((f32[256,256]{0,1:T(8,128)}), f32[256,256]{0,1:T(8,128)}) %all-reduce.23.cloned.1.call-update) | async-done | bytes 262160 | tf_op jit(solution)/shard_map/psum | solution.py:12
  878.9 11.7 cholesky.240
  890.7 9.8 custom-call.19
  901.0 11.7 cholesky.257
  915.4 4.3 while.11
  916.4 1.3 bitcast_dynamic-update-slice_fusion.9
  918.4 1.3 bitcast_dynamic-update-slice_fusion.9
  919.8 19.7 %custom-call.20 = f32[2,128,128]{1,2,0:T(8,128)S(1)} custom-call(f32[2,128,128]{2,1,0:T(8,128)S(1)} %get-tuple-element.65), custom_call_target="InvertDiagBlocksLowerTriangular" | custom-call | tf_op jit(solution)/shard_map/jit(_solve_triangular)/triangular_solve | solution.py:19
  942.5 1.2 select_select_fusion
  943.8 108.4 %all-reduce.25.cloned.1.call-done = f32[4,256,256]{1,2,0:T(8,128)} async-done(((f32[4,256,256]{1,2,0:T(8,128)}), f32[4,256,256]{1,2,0:T(8,128)}) %all-reduce.25.cloned.1.call-update) | async-done | bytes 1048592 | tf_op jit(solution)/shard_map/psum | solution.py:12
  1053.8 1.2 fusion.1
  1055.0 100.7 %all-reduce.27.cloned.1.call-done = f32[4,256,256]{1,2,0:T(8,128)} async-done(((f32[4,256,256]{1,2,0:T(8,128)}), f32[4,256,256]{1,2,0:T(8,128)}) %all-reduce.27.cloned.1.call-update) | async-done | bytes 1048592 | tf_op jit(solution)/shard_map/psum | solution.py:12
  1155.7 7.5 subtract_select_fusion
  1163.1 5.2 copy.53
  1168.4 5.2 copy.76
  (115 shorter events, 33.8 us)
Async XLA Ops:
  6.5 109.6 %all-reduce.11.cloned.1.call-start = ((), (), s32[]{:S(2)}) async-start(), calls=%async_computation | async-start | bytes 524288 | tf_op jit(solution)/shard_map/psum | solution.py:12
  19.1 271.4 %all-reduce.13.cloned.1.call-start = ((), (), s32[]{:S(2)}) async-start(), calls=%async_computation.1 | async-start | bytes 2097152 | tf_op jit(solution)/shard_map/psum | solution.py:12
  182.2 211.7 %all-reduce.15.cloned.1.call-start = ((), (), s32[]{:S(2)}) async-start(), calls=%async_computation.2 | async-start | bytes 2097152 | tf_op jit(solution)/shard_map/psum | solution.py:12
  290.4 2.0 copy-start.2
  291.5 204.6 %all-reduce.17.cloned.1.call-start = ((), (), s32[]{:S(2)}) async-start(), calls=%async_computation.3 | async-start | bytes 524288 | tf_op jit(solution)/shard_map/psum | solution.py:12
  399.7 2.0 copy-start.1
  402.5 268.7 %all-reduce.19.cloned.1.call-start = ((), (), s32[]{:S(2)}) async-start(), calls=%async_computation.4 | async-start | bytes 2097152 | tf_op jit(solution)/shard_map/psum | solution.py:12
  563.0 211.6 %all-reduce.21.cloned.1.call-start = ((), (), s32[]{:S(2)}) async-start(), calls=%async_computation.5 | async-start | bytes 2097152 | tf_op jit(solution)/shard_map/psum | solution.py:12
  671.2 1.6 copy-start.3
  672.3 204.5 %all-reduce.23.cloned.1.call-start = ((), (), s32[]{:S(2)}) async-start(), calls=%async_computation.6 | async-start | bytes 524288 | tf_op jit(solution)/shard_map/psum | solution.py:12
  780.3 2.0 copy-start
  783.1 269.1 %all-reduce.25.cloned.1.call-start = ((), (), s32[]{:S(2)}) async-start(), calls=%async_computation.7 | async-start | bytes 2097152 | tf_op jit(solution)/shard_map/psum | solution.py:12
  943.8 211.9 %all-reduce.27.cloned.1.call-start = ((), (), s32[]{:S(2)}) async-start(), calls=%async_computation.8 | async-start | bytes 2097152 | tf_op jit(solution)/shard_map/psum | solution.py:12
  1052.2 1.6 copy-start.4
Sparse Core Ops, SparseCore 0:
  19.2 96.8 all-reduce.10
  182.3 108.0 all-reduce.12
  293.7 100.1 all-reduce.14
  402.6 93.4 all-reduce.16
  563.1 108.0 all-reduce.18
  674.3 100.1 all-reduce.20
  783.2 93.5 all-reduce.22
  943.9 108.2 all-reduce.24
  1055.4 100.1 all-reduce.26
where the time goes:
time: 1190 us; the launch traced here: 1180 us
  waiting for transfers between devices  903 us (76%)
  other arithmetic  179 us (15%)
  local copies, waits for them, and re-layouts  50.7 us (4%)
  matrix products  27.3 us (2%)
  between operations  18 us (2%)
    psum x9, waiting for transfers between devices, from_root(): return lax.psum(jnp.where(mine, shard, jnp.zeros_like(shard)), axis)  903 us
    another operation x20, other arithmetic, body(): factor = jnp.linalg.cholesky(diag_block)  103 us
    another operation x7, other arithmetic, solve_panel(): solved = jax.scipy.linalg.solve_triangular(factor, flat.T, lower=True).T  59.1 us
  transfers between devices with their start and end apart: 9, of which 9 were waited for; matrix products, arithmetic and copies ran while one was open for 1% of the time, Pallas kernels for 0%

commit v1 on v0

--- a/solution.py
+++ b/solution.py
@@ -9,7 +9,7 @@
 
 def from_root(shard, axis, root):
     mine = lax.axis_index(axis) == root
-    return lax.psum(jnp.where(mine, shard, jnp.zeros_like(shard)), axis)
+    return jnp.sum(lax.all_gather(jnp.where(mine, shard, jnp.zeros_like(shard)), axis), axis=0)
 
 
 def solve_panel(factor, raw_rows):

time: 1190 us -> 1130 us (0.950)
  waiting for transfers between devices: 903 us -> 790 us
  other arithmetic: 179 us -> 227 us
    psum x9 -> x0, waiting for transfers between devices: 903 us -> none  [from_root(): return lax.psum(jnp.where(mine, shard, jnp.zeros_like(shard)), axis)]
    all_gather x0 -> x9, waiting for transfers between devices: none -> 790 us  [from_root(): lax.all_gather(jnp.where(mine, shard, jnp.zeros_like(shard)), axis)]
    reduce_sum x0 -> x9, other arithmetic: none -> 49.4 us  [from_root(): jnp.sum(lax.all_gather(jnp.where(mine, shard, jnp.zeros_like(shard)), axi...]
where the time goes in v1:
time: 1130 us; the launch traced here: 1110 us
  waiting for transfers between devices  790 us (70%)
  other arithmetic  227 us (20%)
  local copies, waits for them, and re-layouts  44.1 us (4%)
  matrix products  33.7 us (3%)
  between operations  17.9 us (2%)
    all_gather x9, waiting for transfers between devices, from_root(): lax.all_gather(jnp.where(mine, shard, jnp.zeros_like(shard)), axis)  790 us
    another operation x20, other arithmetic, body(): factor = jnp.linalg.cholesky(diag_block)  103 us
    another operation x7, other arithmetic, solve_panel(): solved = jax.scipy.linalg.solve_triangular(factor, flat.T, lower=True).T  59.1 us
    reduce_sum x9, other arithmetic, from_root(): jnp.sum(lax.all_gather(jnp.where(mine, shard, jnp.zeros_like(shard)), axi...  49.4 us
    dot_general x3, matrix products, subtract(): jnp.einsum('lan,mbn->lamb', panel_rows, column_rows, precision=lax.Precis...  26.7 us
  transfers between devices with their start and end apart: 9, of which 9 were waited for; matrix products, arithmetic and copies ran while one was open for 1% of the time, Pallas kernels for 0%

profile of v1, /device:TPU:32, one launch (start us, length us, event | category | flops | bytes accessed | tf_op | source)
XLA Modules:
  0.0 1114.5 jit_solution(9293597710394804832)
XLA Ops:
  6.5 5.6 reshape.347
  12.1 4.9 copy.27
  17.0 1.7 slice_select_fusion.2
  20.4 57.6 %all-gather.22.cloned.1.call-done = f32[16,256,1,256]{3,1,2,0:T(8,128)} async-done(((f32[1,256,1,256]{3,1,2,0:T(8,128)}), f32[16,256,1,256]{3,1,2,0:T(8,128)}) %all-gather.22.cloned.1.call-update) | async-done | bytes 4194320 | tf_op jit(solution)/shard_map/all_gather | solution.py:12
  78.0 2.5 reduce_sum.87
  80.7 11.7 %cholesky.172 = f32[128,128]{1,0:T(8,128)S(1)} custom-call(f32[128,128]{1,0:T(8,128)S(1)} %cholesky.270), custom_call_target="Cholesky" | custom-call | tf_op jit(solution)/shard_map/jit(cholesky)/cholesky | solution.py:53
  92.5 9.8 custom-call.15
  102.7 11.7 %cholesky.189 = f32[128,128]{1,0:T(8,128)S(1)} custom-call(f32[128,128]{1,0:T(8,128)S(1)} %convolution_subtract_fusion.7), custom_call_target="Cholesky" | custom-call | tf_op jit(solution)/shard_map/jit(cholesky)/cholesky | solution.py:53
  116.7 4.6 while.9
  117.8 1.4 bitcast_dynamic-update-slice_fusion.6
  119.8 1.4 bitcast_dynamic-update-slice_fusion.6
  121.3 19.7 %custom-call.16 = f32[2,128,128]{1,2,0:T(8,128)S(1)} custom-call(f32[2,128,128]{2,1,0:T(8,128)S(1)} %get-tuple-element.63), custom_call_target="InvertDiagBlocksLowerTriangular" | custom-call | tf_op jit(solution)/shard_map/jit(_solve_triangular)/triangular_solve | solution.py:19
  144.5 93.3 %all-gather.16.cloned.1.call-done = f32[16,4,256,256]{3,2,1,0:T(8,128)} async-done(((f32[1,4,256,256]{3,2,1,0:T(8,128)}), f32[16,4,256,256]{3,2,1,0:T(8,128)}) %all-gather.16.cloned.1.call-update) | async-done | bytes 16777232 | tf_op jit(solution)/shard_map/all_gather | solution.py:12
  237.8 7.0 reduce_sum.88
  246.9 2.4 fusion.11
  249.4 114.5 %all-gather.24.cloned.1.call-done = f32[64,256,256]{2,1,0:T(8,128)} async-done(((f32[4,256,256]{2,1,0:T(8,128)}), f32[64,256,256]{2,1,0:T(8,128)}) %all-gather.24.cloned.1.call-update) | async-done | bytes 16777232 | tf_op jit(solution)/shard_map/all_gather | solution.py:12
  363.8 7.0 reduce_sum.90
  370.8 8.7 convolution_subtract_fusion.1
  379.5 2.0 copy-done.1
  384.1 54.5 %all-gather.26.cloned.1.call-done = f32[16,256,1,256]{3,1,2,0:T(8,128)} async-done(((f32[1,256,1,256]{3,1,2,0:T(8,128)}), f32[16,256,1,256]{3,1,2,0:T(8,128)}) %all-gather.26.cloned.1.call-update) | async-done | bytes 4194320 | tf_op jit(solution)/shard_map/all_gather | solution.py:12
  438.7 2.5 reduce_sum.91
  441.4 11.7 %cholesky.206 = f32[128,128]{1,0:T(8,128)S(1)} custom-call(f32[128,128]{1,0:T(8,128)S(1)} %cholesky.273), custom_call_target="Cholesky" | custom-call | tf_op jit(solution)/shard_map/jit(cholesky)/cholesky | solution.py:53
  453.1 9.8 custom-call.17
  463.4 11.7 %cholesky.223 = f32[128,128]{1,0:T(8,128)S(1)} custom-call(f32[128,128]{1,0:T(8,128)S(1)} %convolution_subtract_fusion.6), custom_call_target="Cholesky" | custom-call | tf_op jit(solution)/shard_map/jit(cholesky)/cholesky | solution.py:53
  477.8 4.3 while.10
  482.1 19.7 %custom-call.18 = f32[2,128,128]{1,2,0:T(8,128)S(1)} custom-call(f32[2,128,128]{2,1,0:T(8,128)S(1)} %get-tuple-element.64), custom_call_target="InvertDiagBlocksLowerTriangular" | custom-call | tf_op jit(solution)/shard_map/jit(_solve_triangular)/triangular_solve | solution.py:19
  505.4 93.3 %all-gather.18.cloned.1.call-done = f32[16,4,256,256]{3,2,1,0:T(8,128)} async-done(((f32[1,4,256,256]{3,2,1,0:T(8,128)}), f32[16,4,256,256]{3,2,1,0:T(8,128)}) %all-gather.18.cloned.1.call-update) | async-done | bytes 16777232 | tf_op jit(solution)/shard_map/all_gather | solution.py:12
  598.7 7.0 reduce_sum.92
  607.8 2.4 fusion.7
  610.3 114.5 %all-gather.28.cloned.1.call-done = f32[64,256,256]{2,1,0:T(8,128)} async-done(((f32[4,256,256]{2,1,0:T(8,128)}), f32[64,256,256]{2,1,0:T(8,128)}) %all-gather.28.cloned.1.call-update) | async-done | bytes 16777232 | tf_op jit(solution)/shard_map/all_gather | solution.py:12
  724.7 7.0 reduce_sum.94
  731.7 8.7 convolution_subtract_fusion
  740.4 2.0 copy-done
  745.3 54.3 %all-gather.30.cloned.1.call-done = f32[16,256,1,256]{3,1,2,0:T(8,128)} async-done(((f32[1,256,1,256]{3,1,2,0:T(8,128)}), f32[16,256,1,256]{3,1,2,0:T(8,128)}) %all-gather.30.cloned.1.call-update) | async-done | bytes 4194320 | tf_op jit(solution)/shard_map/all_gather | solution.py:12
  799.6 2.5 reduce_sum.95
  802.3 11.7 %cholesky.240 = f32[128,128]{1,0:T(8,128)S(1)} custom-call(f32[128,128]{1,0:T(8,128)S(1)} %cholesky.276), custom_call_target="Cholesky" | custom-call | tf_op jit(solution)/shard_map/jit(cholesky)/cholesky | solution.py:53
  814.0 9.8 custom-call.19
  824.3 11.7 %cholesky.257 = f32[128,128]{1,0:T(8,128)S(1)} custom-call(f32[128,128]{1,0:T(8,128)S(1)} %convolution_subtract_fusion.5), custom_call_target="Cholesky" | custom-call | tf_op jit(solution)/shard_map/jit(cholesky)/cholesky | solution.py:53
  838.8 4.2 while.11
  843.0 19.7 %custom-call.20 = f32[2,128,128]{1,2,0:T(8,128)S(1)} custom-call(f32[2,128,128]{2,1,0:T(8,128)S(1)} %get-tuple-element.65), custom_call_target="InvertDiagBlocksLowerTriangular" | custom-call | tf_op jit(solution)/shard_map/jit(_solve_triangular)/triangular_solve | solution.py:19
  866.3 93.3 %all-gather.20.cloned.1.call-done = f32[16,4,256,256]{3,2,1,0:T(8,128)} async-done(((f32[1,4,256,256]{3,2,1,0:T(8,128)}), f32[16,4,256,256]{3,2,1,0:T(8,128)}) %all-gather.20.cloned.1.call-update) | async-done | bytes 16777232 | tf_op jit(solution)/shard_map/all_gather | solution.py:12
  959.6 7.0 reduce_sum.96
  968.8 2.4 fusion.3
  971.2 114.4 %all-gather.32.cloned.1.call-done = f32[64,256,256]{2,1,0:T(8,128)} async-done(((f32[4,256,256]{2,1,0:T(8,128)}), f32[64,256,256]{2,1,0:T(8,128)}) %all-gather.32.cloned.1.call-update) | async-done | bytes 16777232 | tf_op jit(solution)/shard_map/all_gather | solution.py:12
  1085.6 7.0 reduce_sum.98
  1092.6 9.4 subtract_select_fusion
  1102.0 2.7 copy.44
  1104.7 3.0 copy.61
  (117 shorter events, 39.0 us)
Async XLA Ops:
  6.5 71.5 %all-gather.22.cloned.1.call-start = ((), (), s32[]{:S(2)}) async-start(), calls=%async_computation.3 | async-start | bytes 4456448 | tf_op jit(solution)/shard_map/all_gather | solution.py:12
  18.7 219.1 %all-gather.16.cloned.1.call-start = ((), (), s32[]{:S(2)}) async-start(), calls=%async_computation | async-start | bytes 17825792 | tf_op jit(solution)/shard_map/all_gather | solution.py:12
  144.5 219.4 %all-gather.24.cloned.1.call-start = ((), (), s32[]{:S(2)}) async-start(), calls=%async_computation.4 | async-start | bytes 17825792 | tf_op jit(solution)/shard_map/all_gather | solution.py:12
  246.9 191.8 %all-gather.26.cloned.1.call-start = ((), (), s32[]{:S(2)}) async-start(), calls=%async_computation.5 | async-start | bytes 4456448 | tf_op jit(solution)/shard_map/all_gather | solution.py:12
  379.5 2.0 copy-start.1
  382.3 216.5 %all-gather.18.cloned.1.call-start = ((), (), s32[]{:S(2)}) async-start(), calls=%async_computation.1 | async-start | bytes 17825792 | tf_op jit(solution)/shard_map/all_gather | solution.py:12
  505.3 219.4 %all-gather.28.cloned.1.call-start = ((), (), s32[]{:S(2)}) async-start(), calls=%async_computation.6 | async-start | bytes 17825792 | tf_op jit(solution)/shard_map/all_gather | solution.py:12
  607.8 191.8 %all-gather.30.cloned.1.call-start = ((), (), s32[]{:S(2)}) async-start(), calls=%async_computation.7 | async-start | bytes 4456448 | tf_op jit(solution)/shard_map/all_gather | solution.py:12
  740.4 2.0 copy-start
  743.2 216.4 %all-gather.20.cloned.1.call-start = ((), (), s32[]{:S(2)}) async-start(), calls=%async_computation.2 | async-start | bytes 17825792 | tf_op jit(solution)/shard_map/all_gather | solution.py:12
  866.2 219.4 %all-gather.32.cloned.1.call-start = ((), (), s32[]{:S(2)}) async-start(), calls=%async_computation.8 | async-start | bytes 17825792 | tf_op jit(solution)/shard_map/all_gather | solution.py:12
Sparse Core Ops, SparseCore 0:
  18.8 59.1 all-gather.21
  144.6 93.2 all-gather.15
  247.0 116.7 all-gather.23
  382.4 56.2 all-gather.25
  505.5 93.2 all-gather.17
  607.9 116.7 all-gather.27
  743.3 56.2 all-gather.29
  866.3 93.2 all-gather.19
  968.8 116.7 all-gather.31
